TPU v7x, 32 devices: a whole 2x2x4 slice. The times are simulated.
32 devices in a mesh: pts: 2 (over core), cen: 16 (over z, y, x).
Axes of the slice: x: 2, y: 2, z: 4, core: 2. Of those that a mesh axis runs over, the one named last changes fastest.
Arguments:
- points: bfloat16 [2, 1024, 256], P(None, ('pts', 'cen')), may hold values from -4096 to 4096, as said below
- centroids: float32 [16384, 256], P('cen'), may hold values from -6 to 6, as said below
Outputs:
- new_centroids: float32 [16384, 256], P('cen')
- energy: float32 [2, 1024], P(None, 'pts')
Inputs may be any that keep to these rules, and one draw needn't show every extreme that they name: Real-valued points. Real-valued centroids.
All inputs are finite; a program needn't handle non-finite values.
Results may differ from a plain program's by a relative error of at most 0.0003.
The roundings to bfloat16 on the way count: a program that leaves them out, or rounds other values in their place, can miss the bound.
Values may be sent and summed in bfloat16 or wider, within the bound.
A program may use at most 64 MiB of HBM per device.

v0:
```python
import jax
import jax.numpy as jnp
from jax import lax
from jax.sharding import PartitionSpec as P

STEPS = 2


TEMPER = 32.0


def joined(value, axis, join):
    pieces = jax.tree.map(lambda part: lax.all_gather(part, axis), value)
    head = jax.tree.map(lambda part: part[0], pieces)
    tail = jax.tree.map(lambda part: part[1:], pieces)
    running, _ = lax.scan(lambda running, section: (join(running, section), None), head, tail)
    return running


def combine_softmax(first, second):
    top = jnp.maximum(first[0], second[0])
    total = first[1] * jnp.exp(first[0] - top) + second[1] * jnp.exp(second[0] - top)
    return (top, total)


def on_device(points, centroids):
    current = centroids
    energies = []
    for iteration in range(STEPS):
        cent_low = current.astype(jnp.bfloat16)
        cent_sq = jnp.sum(current * current, axis=1)
        segment = lax.all_gather(points[iteration], "cen", axis=0, tiled=True)
        inner = lax.dot_general(
            segment, cent_low, (((1,), (1,)), ((), ())), preferred_element_type=jnp.float32
        )
        logits = (2.0 * inner - cent_sq[None, :]) / TEMPER
        local_top = jnp.max(logits, axis=1)
        local_weights = jnp.exp(logits - local_top[:, None])
        local_total = jnp.sum(local_weights, axis=1)
        top, total = joined((local_top, local_total), "cen", combine_softmax)
        weights = local_weights * jnp.exp(local_top - top)[:, None]
        resp = weights / total[:, None]
        counts = jnp.sum(resp, axis=0)
        sums = lax.dot_general(
            resp.astype(jnp.bfloat16),
            segment,
            (((0,), (0,)), ((), ())),
            preferred_element_type=jnp.float32,
        )
        sums, counts = lax.psum((sums, counts), "pts")
        current = (current + sums) / (1.0 + counts)[:, None]
        energies.append(top + jnp.log(total))
    return (current, jnp.stack(energies))


def solution(mesh):
    placed = (P(None, ("pts", "cen"), None), P("cen", None))
    return jax.shard_map(
        on_device,
        mesh=mesh,
        in_specs=placed,
        out_specs=(P("cen", None), P(None, "pts")),
        check_vma=False,
    )
```

profile of v0, /device:TPU:0, one launch (start us, length us, event | category | flops | bytes accessed | tf_op | source)
XLA Modules:
  0.0 274.8 jit_solution(6816638734251444056)
XLA Ops:
  7.2 0.0 copy-start
  7.2 0.0 all-reduce.3.cloned.1.call-start
  7.2 1.5 multiply_reduce_fusion.1
  8.7 0.7 fusion.14
  9.5 43.8 %all-gather = bf16[1,512,256]{2,1,0:T(8,128)(2,1)S(1)} all-gather(bf16[1,32,256]{2,1,0:T(8,128)(2,1)S(1)} %get-tuple-element.95), channel_id=2, replica_groups=mesh['pts'=2,'cen'=16] {'cen'}, dimensions={1}, use_global_device_ids=true | all-gather | bytes 278528 | tf_op jit(solution)/shard_map/all_gather | solution.py:32
  53.3 0.6 fusion.15
  53.8 0.5 fusion
  54.3 35.6 %all-gather.7 = f32[16,1,512]{2,1,0:T(1,128)S(1)} all-gather(f32[1,1,512]{2,1,0:T(1,128)S(1)} %bitcast.65), channel_id=4, replica_groups=mesh['pts'=2,'cen'=16] {'cen'}, dimensions={0}, use_global_device_ids=true | all-gather | bytes 34816 | tf_op jit(solution)/shard_map/all_gather | solution.py:13
  89.9 37.6 %all-gather.6 = f32[16,1,512]{2,1,0:T(1,128)S(1)} all-gather(f32[1,1,512]{2,1,0:T(1,128)S(1)} %bitcast.62), channel_id=3, replica_groups=mesh['pts'=2,'cen'=16] {'cen'}, dimensions={0}, use_global_device_ids=true | all-gather | bytes 34816 | tf_op jit(solution)/shard_map/all_gather | solution.py:13
  127.6 0.8 while.24
  128.4 0.6 fusion.13
  129.0 1.5 fusion.4
  130.4 0.0 all-reduce.3.cloned.1.call-update
  130.4 0.0 all-reduce.5.cloned.1.call-start
  130.5 2.5 psum.29
  133.0 36.8 %all-gather.3 = bf16[1,512,256]{2,1,0:T(8,128)(2,1)S(1)} all-gather(bf16[1,32,256]{2,1,0:T(8,128)(2,1)S(1)} %get-tuple-element.94), channel_id=5, replica_groups=mesh['pts'=2,'cen'=16] {'cen'}, dimensions={1}, use_global_device_ids=true | all-gather | bytes 278528 | tf_op jit(solution)/shard_map/all_gather | solution.py:32
  169.8 1.6 multiply_reduce_fusion
  171.4 0.0 copy-start.1
  171.4 0.5 fusion.16
  171.9 0.4 fusion.1
  172.3 0.1 copy-done.1
  172.4 37.7 %all-gather.9 = f32[16,1,512]{2,1,0:T(1,128)S(1)} all-gather(f32[1,1,512]{2,1,0:T(1,128)S(1)} %bitcast.66), channel_id=7, replica_groups=mesh['pts'=2,'cen'=16] {'cen'}, dimensions={0}, use_global_device_ids=true | all-gather | bytes 34816 | tf_op jit(solution)/shard_map/all_gather | solution.py:13
  210.1 35.6 %all-gather.8 = f32[16,1,512]{2,1,0:T(1,128)S(1)} all-gather(f32[1,1,512]{2,1,0:T(1,128)S(1)} %bitcast.61), channel_id=6, replica_groups=mesh['pts'=2,'cen'=16] {'cen'}, dimensions={0}, use_global_device_ids=true | all-gather | bytes 34816 | tf_op jit(solution)/shard_map/all_gather | solution.py:13
  245.7 0.8 while.25
  246.6 1.6 fusion.2
  248.2 0.0 all-reduce.5.cloned.1.call-update
  248.2 0.5 fusion.8
  248.7 2.5 psum.31
  251.2 0.6 pad_maximum_fusion
  251.8 13.8 %all-reduce.5.cloned.1.call-done = f32[1024,256]{1,0:T(8,128)} async-done(((f32[1024,256]{1,0:T(8,128)}), f32[1024,256]{1,0:T(8,128)}) %all-reduce.5.cloned.1.call-update) | async-done | bytes 1048592 | tf_op jit(solution)/shard_map/psum | solution.py:50
  265.6 0.0 copy-done.2
  265.6 2.4 add_divide_fusion
  (79 shorter events, 1.0 us)
Async XLA Ops:
  7.2 46.1 %copy-start = (f32[1024,256]{1,0:T(8,128)S(1)}, f32[1024,256]{1,0:T(8,128)}, u32[]{:S(2)}) copy-start(f32[1024,256]{1,0:T(8,128)} %param.7) | copy-start | bytes 3145732
  7.2 162.7 %all-reduce.3.cloned.1.call-start = ((), (), s32[]{:S(2)}) async-start(), calls=%async_computation | async-start | bytes 2097152 | tf_op jit(solution)/shard_map/psum | solution.py:50
  130.4 135.1 %all-reduce.5.cloned.1.call-start = ((), (), s32[]{:S(2)}) async-start(), calls=%async_computation.1 | async-start | bytes 2097152 | tf_op jit(solution)/shard_map/psum | solution.py:50
  171.4 1.0 copy-start.1
  248.2 17.4 %copy-start.2 = (f32[1024,256]{1,0:T(8,128)S(1)}, f32[1024,256]{1,0:T(8,128)}, u32[]{:S(2)}) copy-start(f32[1024,256]{1,0:T(8,128)} %copy-done.1) | copy-start | bytes 3145732
Sparse Core Ops, SparseCore 0:
  130.6 15.2 all-reduce.2
  248.3 17.1 all-reduce.4
where the time goes:
time: 275 us
  blocking collectives  232 us (84%)
  between operations  14.1 us (5%)
  waiting for transfers between devices  13.8 us (5%)
  other arithmetic  8.64 us (3%)
  matrix products  4.11 us (1%)
    all_gather x4, blocking collectives, joined(): pieces = jax.tree.map(lambda part: lax.all_gather(part, axis), value)  147 us
    all_gather x2, blocking collectives, on_device(): segment = lax.all_gather(points[iteration], 'cen', axis=0, tiled=True)  80.6 us
    psum x2, waiting for transfers between devices, on_device(): sums, counts = lax.psum((sums, counts), 'pts')  13.8 us
  transfers between devices with their start and end apart: 2, of which 1 were waited for; matrix products, arithmetic and copies ran while one was open for 0% of the time, Pallas kernels for 0%

commit v1 on v0

v1 whole, which is shorter than its diff:
```python
import functools

import jax
import jax.numpy as jnp
from jax import lax
from jax.experimental import pallas as pl
from jax.experimental.pallas import tpu as pltpu
from jax.sharding import PartitionSpec as P

TEMPER = 32.0
MESH = pl.DeviceIdType.MESH
LANES = 128
ROWS = 256


def split(n):
    near = 1
    while near * near * 4 <= n:
        near *= 2
    if n % near:
        near = 1
    return n // near, near


def kernel(far, near, n_pts, pts_ref, cen_ref, out_ref, en_ref,
           x_ref, w_ref, cur_ref, low_ref, sq_ref, stat1, stat2, got,
           z_send, q_send, p_recv, s1_send, s1_recv, s2_send, s2_recv, c_send, c_recv):
    steps, own, dim = pts_ref.shape
    k_loc = cen_ref.shape[0]
    n_blk = k_loc // ROWS
    width = near * own
    cols = width // LANES
    groups = far * cols
    cen = lax.axis_index("cen")
    p = lax.axis_index("pts")
    a = cen // near
    b = lax.rem(cen, near)
    far_peers = [lax.rem(a + d, far) for d in range(1, far)]
    near_peers = [lax.rem(b + d, near) for d in range(1, near)]
    pts_peers = [lax.rem(p + d, n_pts) for d in range(1, n_pts)]

    barrier = pltpu.get_barrier_semaphore()
    for peer in far_peers:
        pl.semaphore_signal(barrier, inc=1, device_id={"cen": peer * near + b}, device_id_type=MESH)
    for peer in near_peers:
        pl.semaphore_signal(barrier, inc=1, device_id={"cen": a * near + peer}, device_id_type=MESH)
    for peer in pts_peers:
        pl.semaphore_signal(barrier, inc=1, device_id={"pts": peer}, device_id_type=MESH)

    def prepare(rows, value):
        cur_ref[rows, :] = value
        low = value.astype(jnp.bfloat16).astype(jnp.float32) * (2.0 / TEMPER)
        low_ref[rows, :] = low.astype(jnp.bfloat16)
        sq = jnp.sum(value * value, axis=1, keepdims=True) * (1.0 / TEMPER)
        sq_ref[rows, :] = jnp.broadcast_to(sq, (ROWS, LANES))

    for s in range(steps):
        x_ref[s, a, pl.ds(b * own, own), :] = pts_ref[s]

    @pl.loop(0, n_blk)
    def _(blk):
        rows = pl.ds(pl.multiple_of(blk * ROWS, ROWS), ROWS)
        prepare(rows, cen_ref[rows, :])

    pl.semaphore_wait(barrier, len(far_peers) + len(near_peers) + len(pts_peers))

    def chunk(s, i, j):
        return x_ref.at[s, i, pl.ds(j * own, own), :]

    def far_copy(s, d):
        peer = lax.rem(a + d, far)
        return pltpu.make_async_remote_copy(
            src_ref=pts_ref.at[s], dst_ref=chunk(s, a, b),
            send_sem=z_send.at[s, d], recv_sem=p_recv.at[s, a, b],
            device_id={"cen": peer * near + b}, device_id_type=MESH)

    def near_copy(s, i, d):
        peer = lax.rem(b + d, near)
        return pltpu.make_async_remote_copy(
            src_ref=chunk(s, i, b), dst_ref=chunk(s, i, b),
            send_sem=q_send.at[s, i, d], recv_sem=p_recv.at[s, i, b],
            device_id={"cen": a * near + peer}, device_id_type=MESH)

    def own_near_copy(s, d):
        peer = lax.rem(b + d, near)
        return pltpu.make_async_remote_copy(
            src_ref=pts_ref.at[s], dst_ref=chunk(s, a, b),
            send_sem=q_send.at[s, a, d], recv_sem=p_recv.at[s, a, b],
            device_id={"cen": a * near + peer}, device_id_type=MESH)

    def arrived(s, i, j):
        pltpu.make_async_remote_copy(
            src_ref=chunk(s, i, j), dst_ref=chunk(s, i, j),
            send_sem=z_send.at[s, 0], recv_sem=p_recv.at[s, i, j],
            device_id={"cen": cen}, device_id_type=MESH).wait_recv()

    def send_own(s):
        for d in range(1, far):
            far_copy(s, d).start()
        for d in range(1, near):
            own_near_copy(s, d).start()

    def forward(s):
        for d in range(1, far):
            i = lax.rem(a - d + far, far)
            arrived(s, i, b)
            for e in range(1, near):
                near_copy(s, i, e).start()

    def stat1_copy(s, d):
        peer = lax.rem(a + d, far)
        return pltpu.make_async_remote_copy(
            src_ref=stat1.at[s, a], dst_ref=stat1.at[s, a],
            send_sem=s1_send.at[s, d], recv_sem=s1_recv.at[s, a],
            device_id={"cen": peer * near + b}, device_id_type=MESH)

    def stat2_copy(s, d):
        peer = lax.rem(b + d, near)
        return pltpu.make_async_remote_copy(
            src_ref=stat2.at[s, b], dst_ref=stat2.at[s, b],
            send_sem=s2_send.at[s, d], recv_sem=s2_recv.at[s, b],
            device_id={"cen": a * near + peer}, device_id_type=MESH)

    def sums_copy(s, d, blk):
        peer = lax.rem(p + d, n_pts)
        return pltpu.make_async_remote_copy(
            src_ref=got.at[s, p, blk], dst_ref=got.at[s, p, blk],
            send_sem=c_send.at[s, d, blk], recv_sem=c_recv.at[s, p, blk],
            device_id={"pts": peer}, device_id_type=MESH)

    def landed(ref, sem):
        pltpu.make_async_remote_copy(
            src_ref=ref, dst_ref=ref, send_sem=z_send.at[0, 0], recv_sem=sem,
            device_id={"cen": cen}, device_id_type=MESH).wait_recv()

    def joined(stat, s, n):
        top = stat[s, 0, 0]
        for i in range(1, n):
            top = jnp.maximum(top, stat[s, i, 0])
        total = stat[s, 0, 1] * jnp.exp(stat[s, 0, 0] - top)
        for i in range(1, n):
            total = total + stat[s, i, 1] * jnp.exp(stat[s, i, 0] - top)
        return top, total

    send_own(0)
    forward(0)
    send_own(1) if steps > 1 else None

    for s in range(steps):
        def one_group(d, carry):
            i = lax.rem(a + d, far)
            for e in range(1, near):
                arrived(s, i, lax.rem(b + e, near))
            for j in range(cols):
                xg = x_ref[s, i, j * LANES:(j + 1) * LANES, :]
                logits = lax.dot_general(
                    low_ref[...], xg, (((1,), (1,)), ((), ())),
                    preferred_element_type=jnp.float32) - sq_ref[...]
                top = jnp.max(logits, axis=0, keepdims=True)
                weights = jnp.exp(logits - top)
                g = i * cols + j
                w_ref[:, pl.ds(pl.multiple_of(g * LANES, LANES), LANES)] = weights
                stat1[s, a, 0, pl.ds(g, 1), :] = top
                stat1[s, a, 1, pl.ds(g, 1), :] = jnp.sum(weights, axis=0, keepdims=True)
            return carry

        lax.fori_loop(0, far, one_group, 0)
        for d in range(1, far):
            stat1_copy(s, d).start()
        if s + 1 < steps:
            forward(s + 1)
            if s + 2 < steps:
                send_own(s + 2)
        for d in range(1, far):
            i = lax.rem(a - d + far, far)
            landed(stat1.at[s, i], s1_recv.at[s, i])
        top, total = joined(stat1, s, far)
        stat2[s, b, 0] = top
        stat2[s, b, 1] = total
        for d in range(1, near):
            stat2_copy(s, d).start()
        for d in range(1, near):
            i = lax.rem(b - d + near, near)
            landed(stat2.at[s, i], s2_recv.at[s, i])
        top, total = joined(stat2, s, near)
        energy = top + jnp.log(total)
        scale = jnp.exp(stat1[s, a, 0] - top) / total
        for g in range(groups):
            en_ref[s:s + 1, g * LANES:(g + 1) * LANES] = energy[g:g + 1, :]
        scale = jnp.concatenate([scale[g:g + 1, :] for g in range(groups)], axis=1)

        @pl.loop(0, n_blk)
        def _(blk):
            rows = pl.ds(pl.multiple_of(blk * ROWS, ROWS), ROWS)
            resp = w_ref[rows, :] * scale
            part = resp[:, :LANES]
            for g in range(1, groups):
                part = part + resp[:, g * LANES:(g + 1) * LANES]
            count = jnp.sum(jnp.transpose(part), axis=0, keepdims=True)
            xs = x_ref[s].reshape(far * width, dim)
            sums = lax.dot_general(
                resp.astype(jnp.bfloat16), xs, (((1,), (0,)), ((), ())),
                preferred_element_type=jnp.float32)
            got[s, p, blk, :ROWS, :] = sums
            got[s, p, blk, ROWS:ROWS + 1, :] = count
            for d in range(1, n_pts):
                sums_copy(s, d, blk).start()

        @pl.loop(0, n_blk)
        def _(blk):
            rows = pl.ds(pl.multiple_of(blk * ROWS, ROWS), ROWS)
            for d in range(1, n_pts):
                i = lax.rem(p + d, n_pts)
                landed(got.at[s, i, blk], c_recv.at[s, i, blk])
            sums = got[s, 0, blk, :ROWS, :]
            count = got[s, 0, blk, ROWS:ROWS + 1, :]
            for i in range(1, n_pts):
                sums = sums + got[s, i, blk, :ROWS, :]
                count = count + got[s, i, blk, ROWS:ROWS + 1, :]
            column = jnp.transpose(jnp.broadcast_to(1.0 + count, (LANES, ROWS)))
            column = jnp.concatenate([column] * (dim // LANES), axis=1)
            value = (cur_ref[rows, :] + sums) / column
            if s + 1 < steps:
                prepare(rows, value)
            else:
                out_ref[rows, :] = value

    for s in range(steps):
        for d in range(1, far):
            far_copy(s, d).wait_send()
            stat1_copy(s, d).wait_send()
            for e in range(1, near):
                near_copy(s, lax.rem(a + d, far), e).wait_send()
        for d in range(1, near):
            own_near_copy(s, d).wait_send()
            stat2_copy(s, d).wait_send()

        @pl.loop(0, n_blk)
        def _(blk):
            for d in range(1, n_pts):
                sums_copy(s, d, blk).wait_send()


def on_device(far, near, n_pts, points, centroids):
    steps, own, dim = points.shape
    k_loc = centroids.shape[0]
    n_blk = k_loc // ROWS
    batch = far * near * own
    groups = batch // LANES
    vmem = pl.BlockSpec(memory_space=pltpu.VMEM)
    dma = pltpu.SemaphoreType.DMA
    return pl.pallas_call(
        functools.partial(kernel, far, near, n_pts),
        out_shape=(jax.ShapeDtypeStruct((k_loc, dim), jnp.float32),
                   jax.ShapeDtypeStruct((steps, batch), jnp.float32)),
        in_specs=[vmem, vmem],
        out_specs=(vmem, vmem),
        scratch_shapes=[
            pltpu.VMEM((steps, far, near * own, dim), jnp.bfloat16),
            pltpu.VMEM((k_loc, batch), jnp.float32),
            pltpu.VMEM((k_loc, dim), jnp.float32),
            pltpu.VMEM((k_loc, dim), jnp.bfloat16),
            pltpu.VMEM((k_loc, LANES), jnp.float32),
            pltpu.VMEM((steps, far, 2, groups, LANES), jnp.float32),
            pltpu.VMEM((steps, near, 2, groups, LANES), jnp.float32),
            pltpu.VMEM((steps, n_pts, n_blk, ROWS + 8, dim), jnp.float32),
            dma((steps, far)),
            dma((steps, far, near)),
            dma((steps, far, near)),
            dma((steps, far)),
            dma((steps, far)),
            dma((steps, near)),
            dma((steps, near)),
            dma((steps, n_pts, n_blk)),
            dma((steps, n_pts, n_blk)),
        ],
        compiler_params=pltpu.CompilerParams(
            collective_id=0, has_side_effects=True, vmem_limit_bytes=60 * 1024 * 1024),
    )(points, centroids)


def solution(mesh):
    far, near = split(mesh.shape["cen"])
    placed = (P(None, ("pts", "cen"), None), P("cen", None))
    return jax.shard_map(
        functools.partial(on_device, far, near, mesh.shape["pts"]),
        mesh=mesh,
        in_specs=placed,
        out_specs=(P("cen", None), P(None, "pts")),
        check_vma=False,
    )
```

time: 275 us -> 40.8 us (0.15)
  blocking collectives: 232 us -> 0 us
  Pallas kernels: 0 us -> 37 us
  waiting for transfers between devices: 13.8 us -> 0 us
  between operations: 14.1 us -> 0.65 us
  other arithmetic: 8.64 us -> 0 us
  matrix products: 4.11 us -> 0 us
    all_gather x6 -> x0, blocking collectives: 227 us -> none  [the longest x4 147 us: joined(): pieces = jax.tree.map(lambda part: lax.all_gather(part, axis), value)]
    pallas_call x0 -> x1, Pallas kernels: none -> 37 us  [on_device(): pl.pallas_call(functools.partial(kernel, far, near, n_pts), out_shape=(ja...]
    psum x2 -> x0, waiting for transfers between devices: 13.8 us -> none  [on_device(): sums, counts = lax.psum((sums, counts), 'pts')]
    reduce_sum x6 -> x0, other arithmetic: 4.99 us -> none  [the longest x2 3.1 us: on_device(): cent_sq = jnp.sum(current * current, axis=1)]
    psum x2 -> x0, blocking collectives: 4.96 us -> none  [on_device(): sums, counts = lax.psum((sums, counts), 'pts')]
    dot_general x4 -> x0, matrix products: 4.11 us -> none  [the longest x2 3.06 us: on_device(): lax.dot_general(resp.astype(jnp.bfloat16), segment, (((0,), (0,)), ((), (...]
  transfers between devices with their start and end apart: 2 -> 0, of which waited for: 1 -> 0; matrix products, arithmetic and copies ran while one was open for 0% -> 0% of each run, Pallas kernels for 0% -> 0%
where the time goes in v1:
time: 40.8 us; the launch traced here: 40.5 us
  Pallas kernels  37 us (91%)
  local copies, waits for them, and re-layouts  2.86 us (7%)
  between operations  0.65 us (2%)
    pallas_call x1, Pallas kernels, on_device(): pl.pallas_call(functools.partial(kernel, far, near, n_pts), out_shape=(ja...  37 us
    unnamed x4, local copies, waits for them, and re-layouts  2.86 us

profile of v1, /device:TPU:0, one launch (start us, length us, event | category | flops | bytes accessed | tf_op | source)
XLA Modules:
  0.0 40.5 jit_solution(9373178148079527314)
XLA Ops:
  0.6 37.0 %shard_map.41 = (f32[1024,256]{1,0:T(8,128)}, f32[2,512]{1,0:T(2,128)}) custom-call(bf16[2,32,256]{2,1,0:T(8,128)(2,1)} %pts_ref.1, f32[1024,256]{1,0:T(8,128)} %cen_ref.1), custom_call_target="tpu_custom_call" | custom-call | tf_op jit(solution)/shard_map/pallas_call | solution.py:252
  37.7 0.0 copy-start
  37.7 2.3 %copy.6 = f32[1024,256]{1,0:T(8,128)} copy(f32[1024,256]{1,0:T(8,128)} %get-tuple-element.4) | data formatting | bytes 2097152
  39.9 0.0 copy-done
  39.9 0.6 %copy.7 = f32[2,512]{1,0:T(2,128)} copy(f32[2,512]{1,0:T(2,128)S(1)} %copy-done) | data formatting | bytes 8192
Async XLA Ops:
  37.7 2.3 %copy-start = (f32[2,512]{1,0:T(2,128)S(1)}, f32[2,512]{1,0:T(2,128)}, u32[]{:S(2)}) copy-start(f32[2,512]{1,0:T(2,128)} %get-tuple-element.5) | copy-start | bytes 12292

commit v2 on v1

--- a/solution.py
+++ b/solution.py
@@ -17,14 +17,23 @@
     near = 1
     while near * near * 4 <= n:
         near *= 2
-    if n % near:
-        near = 1
+    assert n % near == 0 and (n // near) & (n // near - 1) == 0
     return n // near, near
+
+
+def flip(i, d):
+    bit = 1
+    while bit <= d:
+        if d & bit:
+            i = i + bit - 2 * bit * lax.rem(i // bit, 2)
+        bit *= 2
+    return i
 
 
 def kernel(far, near, n_pts, pts_ref, cen_ref, out_ref, en_ref,
            x_ref, w_ref, cur_ref, low_ref, sq_ref, stat1, stat2, got,
-           z_send, q_send, p_recv, s1_send, s1_recv, s2_send, s2_recv, c_send, c_recv):
+           z_send, q_send, p_recv, s1_send, s1_recv, s2_send, s2_recv, c_send, c_recv,
+           in_sem, cen_sem):
     steps, own, dim = pts_ref.shape
     k_loc = cen_ref.shape[0]
     n_blk = k_loc // ROWS
@@ -35,8 +44,8 @@
     p = lax.axis_index("pts")
     a = cen // near
     b = lax.rem(cen, near)
-    far_peers = [lax.rem(a + d, far) for d in range(1, far)]
-    near_peers = [lax.rem(b + d, near) for d in range(1, near)]
+    far_peers = [flip(a, d) for d in range(1, far)]
+    near_peers = [flip(b, d) for d in range(1, near)]
     pts_peers = [lax.rem(p + d, n_pts) for d in range(1, n_pts)]
 
     barrier = pltpu.get_barrier_semaphore()
@@ -48,19 +57,33 @@
         pl.semaphore_signal(barrier, inc=1, device_id={"pts": peer}, device_id_type=MESH)
 
     def prepare(rows, value):
-        cur_ref[rows, :] = value
         low = value.astype(jnp.bfloat16).astype(jnp.float32) * (2.0 / TEMPER)
         low_ref[rows, :] = low.astype(jnp.bfloat16)
         sq = jnp.sum(value * value, axis=1, keepdims=True) * (1.0 / TEMPER)
         sq_ref[rows, :] = jnp.broadcast_to(sq, (ROWS, LANES))
 
+    def cen_copy(blk):
+        rows = pl.ds(pl.multiple_of(blk * ROWS, ROWS), ROWS)
+        return pltpu.make_async_copy(cen_ref.at[rows, :], cur_ref.at[rows, :], cen_sem.at[blk])
+
+    def pts_copy(s):
+        return pltpu.make_async_copy(pts_ref.at[s], x_ref.at[s, a, pl.ds(b * own, own), :], in_sem.at[s])
+
     for s in range(steps):
-        x_ref[s, a, pl.ds(b * own, own), :] = pts_ref[s]
+        pts_copy(s).start()
 
     @pl.loop(0, n_blk)
     def _(blk):
+        cen_copy(blk).start()
+
+    for s in range(steps):
+        pts_copy(s).wait()
+
+    @pl.loop(0, n_blk)
+    def _(blk):
+        cen_copy(blk).wait()
         rows = pl.ds(pl.multiple_of(blk * ROWS, ROWS), ROWS)
-        prepare(rows, cen_ref[rows, :])
+        prepare(rows, cur_ref[rows, :])
 
     pl.semaphore_wait(barrier, len(far_peers) + len(near_peers) + len(pts_peers))
 
@@ -68,23 +91,23 @@
         return x_ref.at[s, i, pl.ds(j * own, own), :]
 
     def far_copy(s, d):
-        peer = lax.rem(a + d, far)
-        return pltpu.make_async_remote_copy(
-            src_ref=pts_ref.at[s], dst_ref=chunk(s, a, b),
+        peer = flip(a, d)
+        return pltpu.make_async_remote_copy(
+            src_ref=chunk(s, a, b), dst_ref=chunk(s, a, b),
             send_sem=z_send.at[s, d], recv_sem=p_recv.at[s, a, b],
             device_id={"cen": peer * near + b}, device_id_type=MESH)
 
     def near_copy(s, i, d):
-        peer = lax.rem(b + d, near)
+        peer = flip(b, d)
         return pltpu.make_async_remote_copy(
             src_ref=chunk(s, i, b), dst_ref=chunk(s, i, b),
             send_sem=q_send.at[s, i, d], recv_sem=p_recv.at[s, i, b],
             device_id={"cen": a * near + peer}, device_id_type=MESH)
 
     def own_near_copy(s, d):
-        peer = lax.rem(b + d, near)
-        return pltpu.make_async_remote_copy(
-            src_ref=pts_ref.at[s], dst_ref=chunk(s, a, b),
+        peer = flip(b, d)
+        return pltpu.make_async_remote_copy(
+            src_ref=chunk(s, a, b), dst_ref=chunk(s, a, b),
             send_sem=q_send.at[s, a, d], recv_sem=p_recv.at[s, a, b],
             device_id={"cen": a * near + peer}, device_id_type=MESH)
 
@@ -95,27 +118,27 @@
             device_id={"cen": cen}, device_id_type=MESH).wait_recv()
 
     def send_own(s):
-        for d in range(1, far):
+        for d in reversed(range(1, far)):
             far_copy(s, d).start()
-        for d in range(1, near):
+        for d in reversed(range(1, near)):
             own_near_copy(s, d).start()
 
     def forward(s):
         for d in range(1, far):
-            i = lax.rem(a - d + far, far)
+            i = flip(a, d)
             arrived(s, i, b)
-            for e in range(1, near):
+            for e in reversed(range(1, near)):
                 near_copy(s, i, e).start()
 
     def stat1_copy(s, d):
-        peer = lax.rem(a + d, far)
+        peer = flip(a, d)
         return pltpu.make_async_remote_copy(
             src_ref=stat1.at[s, a], dst_ref=stat1.at[s, a],
             send_sem=s1_send.at[s, d], recv_sem=s1_recv.at[s, a],
             device_id={"cen": peer * near + b}, device_id_type=MESH)
 
     def stat2_copy(s, d):
-        peer = lax.rem(b + d, near)
+        peer = flip(b, d)
         return pltpu.make_async_remote_copy(
             src_ref=stat2.at[s, b], dst_ref=stat2.at[s, b],
             send_sem=s2_send.at[s, d], recv_sem=s2_recv.at[s, b],
@@ -147,10 +170,9 @@
     send_own(1) if steps > 1 else None
 
     for s in range(steps):
-        def one_group(d, carry):
-            i = lax.rem(a + d, far)
+        def one_group(i):
             for e in range(1, near):
-                arrived(s, i, lax.rem(b + e, near))
+                arrived(s, i, flip(b, e))
             for j in range(cols):
                 xg = x_ref[s, i, j * LANES:(j + 1) * LANES, :]
                 logits = lax.dot_general(
@@ -162,25 +184,25 @@
                 w_ref[:, pl.ds(pl.multiple_of(g * LANES, LANES), LANES)] = weights
                 stat1[s, a, 0, pl.ds(g, 1), :] = top
                 stat1[s, a, 1, pl.ds(g, 1), :] = jnp.sum(weights, axis=0, keepdims=True)
-            return carry
-
-        lax.fori_loop(0, far, one_group, 0)
-        for d in range(1, far):
+
+        for d in range(far):
+            one_group(flip(a, d))
+        for d in reversed(range(1, far)):
             stat1_copy(s, d).start()
         if s + 1 < steps:
             forward(s + 1)
             if s + 2 < steps:
                 send_own(s + 2)
         for d in range(1, far):
-            i = lax.rem(a - d + far, far)
+            i = flip(a, d)
             landed(stat1.at[s, i], s1_recv.at[s, i])
         top, total = joined(stat1, s, far)
         stat2[s, b, 0] = top
         stat2[s, b, 1] = total
-        for d in range(1, near):
+        for d in reversed(range(1, near)):
             stat2_copy(s, d).start()
         for d in range(1, near):
-            i = lax.rem(b - d + near, near)
+            i = flip(b, d)
             landed(stat2.at[s, i], s2_recv.at[s, i])
         top, total = joined(stat2, s, near)
         energy = top + jnp.log(total)
@@ -221,6 +243,7 @@
             column = jnp.concatenate([column] * (dim // LANES), axis=1)
             value = (cur_ref[rows, :] + sums) / column
             if s + 1 < steps:
+                cur_ref[rows, :] = value
                 prepare(rows, value)
             else:
                 out_ref[rows, :] = value
@@ -230,7 +253,7 @@
             far_copy(s, d).wait_send()
             stat1_copy(s, d).wait_send()
             for e in range(1, near):
-                near_copy(s, lax.rem(a + d, far), e).wait_send()
+                near_copy(s, flip(a, d), e).wait_send()
         for d in range(1, near):
             own_near_copy(s, d).wait_send()
             stat2_copy(s, d).wait_send()
@@ -251,9 +274,9 @@
     dma = pltpu.SemaphoreType.DMA
     return pl.pallas_call(
         functools.partial(kernel, far, near, n_pts),
-        out_shape=(jax.ShapeDtypeStruct((k_loc, dim), jnp.float32),
-                   jax.ShapeDtypeStruct((steps, batch), jnp.float32)),
-        in_specs=[vmem, vmem],
+        out_shape=(pltpu.VMEM((k_loc, dim), jnp.float32),
+                   pltpu.VMEM((steps, batch), jnp.float32)),
+        in_specs=[pl.BlockSpec(memory_space=pl.ANY)] * 2,
         out_specs=(vmem, vmem),
         scratch_shapes=[
             pltpu.VMEM((steps, far, near * own, dim), jnp.bfloat16),
@@ -273,6 +296,8 @@
             dma((steps, near)),
             dma((steps, n_pts, n_blk)),
             dma((steps, n_pts, n_blk)),
+            dma((steps,)),
+            dma((n_blk,)),
         ],
         compiler_params=pltpu.CompilerParams(
             collective_id=0, has_side_effects=True, vmem_limit_bytes=60 * 1024 * 1024),

time: 40.8 us -> 37.7 us (0.924)
  Pallas kernels: 37 us -> 35.1 us
  local copies, waits for them, and re-layouts: 2.86 us -> 1.56 us
    pallas_call x1, Pallas kernels: 37 us -> 35.1 us  [on_device(): pl.pallas_call(functools.partial(kernel, far, near, n_pts), out_shape=(pl...]
    unnamed x4 -> x2, local copies, waits for them, and re-layouts: 2.86 us -> 1.56 us
where the time goes in v2:
time: 37.7 us; the launch traced here: 37.3 us
  Pallas kernels  35.1 us (93%)
  local copies, waits for them, and re-layouts  1.56 us (4%)
  between operations  0.64 us (2%)
    pallas_call x1, Pallas kernels, on_device(): pl.pallas_call(functools.partial(kernel, far, near, n_pts), out_shape=(pl...  35.1 us
    unnamed x2, local copies, waits for them, and re-layouts  1.56 us

profile of v2, /device:TPU:0, one launch (start us, length us, event | category | flops | bytes accessed | tf_op | source)
XLA Modules:
  0.0 37.3 jit_solution(11515869190374722387)
XLA Ops:
  0.6 35.1 %shard_map.41 = (f32[1024,256]{1,0:T(8,128)S(1)}, f32[2,512]{1,0:T(2,128)S(1)}) custom-call(bf16[2,32,256]{2,1,0:T(8,128)(2,1)} %pts_ref.1, f32[1024,256]{1,0:T(8,128)} %cen_ref.1), custom_call_target="tpu_custom_call" | custom-call | tf_op jit(solution)/shard_map/pallas_call | solution.py:275
  35.8 1.0 %copy.6 = f32[1024,256]{1,0:T(8,128)} copy(f32[1024,256]{1,0:T(8,128)S(1)} %get-tuple-element.2) | data formatting | bytes 2097152
  36.7 0.6 %copy.7 = f32[2,512]{1,0:T(2,128)} copy(f32[2,512]{1,0:T(2,128)S(1)} %get-tuple-element.3) | data formatting | bytes 8192

commit v3 on v2

--- a/solution.py
+++ b/solution.py
@@ -31,8 +31,8 @@
 
 
 def kernel(far, near, n_pts, pts_ref, cen_ref, out_ref, en_ref,
-           x_ref, w_ref, cur_ref, low_ref, sq_ref, stat1, stat2, got,
-           z_send, q_send, p_recv, s1_send, s1_recv, s2_send, s2_recv, c_send, c_recv,
+           x_ref, w_ref, cur_ref, low_ref, sq_ref, stat, got,
+           z_send, q_send, p_recv, s_send, s_recv, c_send, c_recv,
            in_sem, cen_sem):
     steps, own, dim = pts_ref.shape
     k_loc = cen_ref.shape[0]
@@ -130,19 +130,11 @@
             for e in reversed(range(1, near)):
                 near_copy(s, i, e).start()
 
-    def stat1_copy(s, d):
-        peer = flip(a, d)
-        return pltpu.make_async_remote_copy(
-            src_ref=stat1.at[s, a], dst_ref=stat1.at[s, a],
-            send_sem=s1_send.at[s, d], recv_sem=s1_recv.at[s, a],
-            device_id={"cen": peer * near + b}, device_id_type=MESH)
-
-    def stat2_copy(s, d):
-        peer = flip(b, d)
-        return pltpu.make_async_remote_copy(
-            src_ref=stat2.at[s, b], dst_ref=stat2.at[s, b],
-            send_sem=s2_send.at[s, d], recv_sem=s2_recv.at[s, b],
-            device_id={"cen": a * near + peer}, device_id_type=MESH)
+    def stat_copy(s, d):
+        return pltpu.make_async_remote_copy(
+            src_ref=stat.at[s, cen], dst_ref=stat.at[s, cen],
+            send_sem=s_send.at[s, d], recv_sem=s_recv.at[s, cen],
+            device_id={"cen": flip(cen, d)}, device_id_type=MESH)
 
     def sums_copy(s, d, blk):
         peer = lax.rem(p + d, n_pts)
@@ -156,14 +148,10 @@
             src_ref=ref, dst_ref=ref, send_sem=z_send.at[0, 0], recv_sem=sem,
             device_id={"cen": cen}, device_id_type=MESH).wait_recv()
 
-    def joined(stat, s, n):
-        top = stat[s, 0, 0]
-        for i in range(1, n):
-            top = jnp.maximum(top, stat[s, i, 0])
-        total = stat[s, 0, 1] * jnp.exp(stat[s, 0, 0] - top)
-        for i in range(1, n):
-            total = total + stat[s, i, 1] * jnp.exp(stat[s, i, 0] - top)
-        return top, total
+    def joined(s):
+        tops = stat[s, :, 0]
+        top = jnp.max(tops, axis=0)
+        return top, jnp.sum(stat[s, :, 1] * jnp.exp(tops - top[None]), axis=0)
 
     send_own(0)
     forward(0)
@@ -182,31 +170,23 @@
                 weights = jnp.exp(logits - top)
                 g = i * cols + j
                 w_ref[:, pl.ds(pl.multiple_of(g * LANES, LANES), LANES)] = weights
-                stat1[s, a, 0, pl.ds(g, 1), :] = top
-                stat1[s, a, 1, pl.ds(g, 1), :] = jnp.sum(weights, axis=0, keepdims=True)
+                stat[s, cen, 0, pl.ds(g, 1), :] = top
+                stat[s, cen, 1, pl.ds(g, 1), :] = jnp.sum(weights, axis=0, keepdims=True)
 
         for d in range(far):
             one_group(flip(a, d))
-        for d in reversed(range(1, far)):
-            stat1_copy(s, d).start()
+        for d in reversed(range(1, far * near)):
+            stat_copy(s, d).start()
         if s + 1 < steps:
             forward(s + 1)
             if s + 2 < steps:
                 send_own(s + 2)
-        for d in range(1, far):
-            i = flip(a, d)
-            landed(stat1.at[s, i], s1_recv.at[s, i])
-        top, total = joined(stat1, s, far)
-        stat2[s, b, 0] = top
-        stat2[s, b, 1] = total
-        for d in reversed(range(1, near)):
-            stat2_copy(s, d).start()
-        for d in range(1, near):
-            i = flip(b, d)
-            landed(stat2.at[s, i], s2_recv.at[s, i])
-        top, total = joined(stat2, s, near)
+        for d in range(1, far * near):
+            i = flip(cen, d)
+            landed(stat.at[s, i], s_recv.at[s, i])
+        top, total = joined(s)
         energy = top + jnp.log(total)
-        scale = jnp.exp(stat1[s, a, 0] - top) / total
+        scale = jnp.exp(stat[s, cen, 0] - top) / total
         for g in range(groups):
             en_ref[s:s + 1, g * LANES:(g + 1) * LANES] = energy[g:g + 1, :]
         scale = jnp.concatenate([scale[g:g + 1, :] for g in range(groups)], axis=1)
@@ -249,14 +229,14 @@
                 out_ref[rows, :] = value
 
     for s in range(steps):
+        for d in range(1, far * near):
+            stat_copy(s, d).wait_send()
         for d in range(1, far):
             far_copy(s, d).wait_send()
-            stat1_copy(s, d).wait_send()
             for e in range(1, near):
                 near_copy(s, flip(a, d), e).wait_send()
         for d in range(1, near):
             own_near_copy(s, d).wait_send()
-            stat2_copy(s, d).wait_send()
 
         @pl.loop(0, n_blk)
         def _(blk):
@@ -284,16 +264,13 @@
             pltpu.VMEM((k_loc, dim), jnp.float32),
             pltpu.VMEM((k_loc, dim), jnp.bfloat16),
             pltpu.VMEM((k_loc, LANES), jnp.float32),
-            pltpu.VMEM((steps, far, 2, groups, LANES), jnp.float32),
-            pltpu.VMEM((steps, near, 2, groups, LANES), jnp.float32),
+            pltpu.VMEM((steps, far * near, 2, groups, LANES), jnp.float32),
             pltpu.VMEM((steps, n_pts, n_blk, ROWS + 8, dim), jnp.float32),
             dma((steps, far)),
             dma((steps, far, near)),
             dma((steps, far, near)),
-            dma((steps, far)),
-            dma((steps, far)),
-            dma((steps, near)),
-            dma((steps, near)),
+            dma((steps, far * near)),
+            dma((steps, far * near)),
             dma((steps, n_pts, n_blk)),
             dma((steps, n_pts, n_blk)),
             dma((steps,)),

time: 37.7 us -> 34.3 us (0.910)
  Pallas kernels: 35.1 us -> 31.9 us
    pallas_call x1, Pallas kernels: 35.1 us -> 31.9 us  [on_device(): pl.pallas_call(functools.partial(kernel, far, near, n_pts), out_shape=(pl...]
where the time goes in v3:
time: 34.3 us; the launch traced here: 34.1 us
  Pallas kernels  31.9 us (93%)
  local copies, waits for them, and re-layouts  1.56 us (5%)
  between operations  0.64 us (2%)
    pallas_call x1, Pallas kernels, on_device(): pl.pallas_call(functools.partial(kernel, far, near, n_pts), out_shape=(pl...  31.9 us
    unnamed x2, local copies, waits for them, and re-layouts  1.56 us

profile of v3, /device:TPU:0, one launch (start us, length us, event | category | flops | bytes accessed | tf_op | source)
XLA Modules:
  0.0 34.1 jit_solution(5096122476829387751)
XLA Ops:
  0.6 31.9 %shard_map.41 = (f32[1024,256]{1,0:T(8,128)S(1)}, f32[2,512]{1,0:T(2,128)S(1)}) custom-call(bf16[2,32,256]{2,1,0:T(8,128)(2,1)} %pts_ref.1, f32[1024,256]{1,0:T(8,128)} %cen_ref.1), custom_call_target="tpu_custom_call" | custom-call | tf_op jit(solution)/shard_map/pallas_call | solution.py:255
  32.5 1.0 %copy.6 = f32[1024,256]{1,0:T(8,128)} copy(f32[1024,256]{1,0:T(8,128)S(1)} %get-tuple-element.2) | data formatting | bytes 2097152
  33.5 0.6 %copy.7 = f32[2,512]{1,0:T(2,128)} copy(f32[2,512]{1,0:T(2,128)S(1)} %get-tuple-element.3) | data formatting | bytes 8192

commit v4 on v3

--- a/solution.py
+++ b/solution.py
@@ -56,11 +56,10 @@
     for peer in pts_peers:
         pl.semaphore_signal(barrier, inc=1, device_id={"pts": peer}, device_id_type=MESH)
 
-    def prepare(rows, value):
+    def lowered(value):
         low = value.astype(jnp.bfloat16).astype(jnp.float32) * (2.0 / TEMPER)
-        low_ref[rows, :] = low.astype(jnp.bfloat16)
         sq = jnp.sum(value * value, axis=1, keepdims=True) * (1.0 / TEMPER)
-        sq_ref[rows, :] = jnp.broadcast_to(sq, (ROWS, LANES))
+        return low.astype(jnp.bfloat16), sq
 
     def cen_copy(blk):
         rows = pl.ds(pl.multiple_of(blk * ROWS, ROWS), ROWS)
@@ -83,7 +82,8 @@
     def _(blk):
         cen_copy(blk).wait()
         rows = pl.ds(pl.multiple_of(blk * ROWS, ROWS), ROWS)
-        prepare(rows, cur_ref[rows, :])
+        low_ref[rows, :], sq = lowered(cur_ref[rows, :])
+        sq_ref[rows, :] = jnp.broadcast_to(sq, (ROWS, LANES))
 
     pl.semaphore_wait(barrier, len(far_peers) + len(near_peers) + len(pts_peers))
 
@@ -173,8 +173,9 @@
                 stat[s, cen, 0, pl.ds(g, 1), :] = top
                 stat[s, cen, 1, pl.ds(g, 1), :] = jnp.sum(weights, axis=0, keepdims=True)
 
-        for d in range(far):
-            one_group(flip(a, d))
+        if s == 0:
+            for d in range(far):
+                one_group(flip(a, d))
         for d in reversed(range(1, far * near)):
             stat_copy(s, d).start()
         if s + 1 < steps:
@@ -208,8 +209,12 @@
             for d in range(1, n_pts):
                 sums_copy(s, d, blk).start()
 
-        @pl.loop(0, n_blk)
-        def _(blk):
+        if s + 1 < steps:
+            for d in range(far):
+                for e in range(1, near):
+                    arrived(s + 1, flip(a, d), flip(b, e))
+
+        def finish(blk, top):
             rows = pl.ds(pl.multiple_of(blk * ROWS, ROWS), ROWS)
             for d in range(1, n_pts):
                 i = lax.rem(p + d, n_pts)
@@ -222,11 +227,29 @@
             column = jnp.transpose(jnp.broadcast_to(1.0 + count, (LANES, ROWS)))
             column = jnp.concatenate([column] * (dim // LANES), axis=1)
             value = (cur_ref[rows, :] + sums) / column
-            if s + 1 < steps:
-                cur_ref[rows, :] = value
-                prepare(rows, value)
-            else:
+            if s + 1 == steps:
                 out_ref[rows, :] = value
+                return top
+            cur_ref[rows, :] = value
+            low, sq = lowered(value)
+            logits = lax.dot_general(
+                low, x_ref[s + 1].reshape(far * width, dim), (((1,), (1,)), ((), ())),
+                preferred_element_type=jnp.float32) - sq
+            w_ref[rows, :] = logits
+            return jnp.maximum(top, jnp.max(logits, axis=0, keepdims=True))
+
+        def weigh(top, blk, total):
+            rows = pl.ds(pl.multiple_of(blk * ROWS, ROWS), ROWS)
+            weights = jnp.exp(w_ref[rows, :] - top)
+            w_ref[rows, :] = weights
+            return total + jnp.sum(weights, axis=0, keepdims=True)
+
+        top = lax.fori_loop(0, n_blk, finish, jnp.full((1, groups * LANES), -jnp.inf, jnp.float32))
+        if s + 1 < steps:
+            total = lax.fori_loop(0, n_blk, functools.partial(weigh, top), jnp.zeros_like(top))
+            for g in range(groups):
+                stat[s + 1, cen, 0, g:g + 1, :] = top[:, g * LANES:(g + 1) * LANES]
+                stat[s + 1, cen, 1, g:g + 1, :] = total[:, g * LANES:(g + 1) * LANES]
 
     for s in range(steps):
         for d in range(1, far * near):

time: 34.3 us -> 32.4 us (0.945)
  Pallas kernels: 31.9 us -> 29.9 us
    pallas_call x1, Pallas kernels: 31.9 us -> 29.9 us  [on_device(): pl.pallas_call(functools.partial(kernel, far, near, n_pts), out_shape=(pl...]
where the time goes in v4:
time: 32.4 us; the launch traced here: 32.1 us
  Pallas kernels  29.9 us (92%)
  local copies, waits for them, and re-layouts  1.56 us (5%)
  between operations  0.64 us (2%)
    pallas_call x1, Pallas kernels, on_device(): pl.pallas_call(functools.partial(kernel, far, near, n_pts), out_shape=(pl...  29.9 us
    unnamed x2, local copies, waits for them, and re-layouts  1.56 us

profile of v4, /device:TPU:0, one launch (start us, length us, event | category | flops | bytes accessed | tf_op | source)
XLA Modules:
  0.0 32.1 jit_solution(13420432417532691248)
XLA Ops:
  0.6 29.9 %shard_map.41 = (f32[1024,256]{1,0:T(8,128)S(1)}, f32[2,512]{1,0:T(2,128)S(1)}) custom-call(bf16[2,32,256]{2,1,0:T(8,128)(2,1)} %pts_ref.1, f32[1024,256]{1,0:T(8,128)} %cen_ref.1), custom_call_target="tpu_custom_call" | custom-call | tf_op jit(solution)/shard_map/pallas_call | solution.py:278
  30.6 1.0 %copy.6 = f32[1024,256]{1,0:T(8,128)} copy(f32[1024,256]{1,0:T(8,128)S(1)} %get-tuple-element.2) | data formatting | bytes 2097152
  31.5 0.6 %copy.7 = f32[2,512]{1,0:T(2,128)} copy(f32[2,512]{1,0:T(2,128)S(1)} %get-tuple-element.3) | data formatting | bytes 8192
